TPU v7x, 256 devices: a whole 4x4x8 slice. The times are simulated.
256 devices in a mesh: sec: 4 (over y_lo, core), mom: 8 (over x, y_hi), en: 8 (over z).
Axes of the slice: x: 4, y: 4 (y_hi: 2, y_lo: 2; y = y_hi * 2 + y_lo), z: 8, core: 2. Of those that a mesh axis runs over, the one named last changes fastest.
Arguments:
- green_blocks: bfloat16 [8, 64, 2, 128, 128], P('mom', ('sec', 'en')), may hold values from -6 to 6
- derivative: bfloat16 [3, 128, 128], replicated, may hold values from -0.5 to 0.5
- bare_phonon: float32 [4, 8, 2, 3, 3, 128], P('sec', 'mom'), may hold values from -4 to 4
- prior_polar: float32 [4, 8, 2, 3, 3, 128], P('sec', 'mom'), may hold values from -4 to 4
- offsets: int32 [4], replicated, may hold values from 1 to 2, as said below
- momenta: int32 [8, 8], replicated, may hold values from 0 to 7, as said below
Outputs:
- sigma: float32 [8, 64, 2, 128, 128], P('mom', ('sec', 'en'))
- polarization: float32 [4, 8, 3, 128], P('sec', 'mom')
Inputs may be any that keep to these rules, and one draw needn't show every extreme that they name: `offsets`: every mode's offset lies in 1 to 2; some mode's offset equals 2 and another mode's equals 1. momenta[k, k'] = p((k - k') mod 8) for a permutation p of the 8 phonon momenta.
All inputs are finite; a program needn't handle non-finite values.
Results may differ from a plain program's by a relative error of at most 0.014.
Values may be sent and summed in bfloat16 or wider, within the bound.
No kernel may reach another device: no remote copies, remote signals or barrier semaphores. Data moves between devices by JAX's collectives and lax.ppermute only.
A program may use at most 64 MiB of HBM per device.

v0:
```python
import math
import jax
import jax.numpy as jnp
from jax import lax
from jax.sharding import PartitionSpec as P


def passed_along(x, axis, by):
    peers = lax.axis_size(axis)
    pairs = [(i, i + by) for i in range(peers) if 0 <= i + by < peers]
    return lax.ppermute(x, axis, pairs)


def contract(former, latter):
    return jnp.sum(former[..., :, :, None, :] * latter[..., None, :, :, :], axis=-3)


def complex_product(former, latter):
    real_part = contract(former[..., 0, :, :, :], latter[..., 0, :, :, :]) - contract(
        former[..., 1, :, :, :], latter[..., 1, :, :, :]
    )
    imag_part = contract(former[..., 0, :, :, :], latter[..., 1, :, :, :]) + contract(
        former[..., 1, :, :, :], latter[..., 0, :, :, :]
    )
    return jnp.stack([real_part, imag_part], axis=-4)


def dyson_update(bare_phonon, prior_polar):
    return bare_phonon + complex_product(complex_product(bare_phonon, prior_polar), bare_phonon)


def flipped_products(blocks, derivative):
    flipped = jnp.einsum(
        "ktcbx,ixa->kticab", blocks, derivative, preferred_element_type=jnp.float32
    )
    sign_flip = jnp.array([1.0, -1.0], jnp.float32).reshape(1, 1, 1, 2, 1, 1)
    return (flipped * sign_flip).astype(jnp.bfloat16)


def mode_weights(chosen):
    real_part = chosen[:, :, 0]
    imag_part = chosen[:, :, 1]
    upper_part = jnp.stack([real_part, -imag_part], axis=2)
    lower_part = jnp.stack([imag_part, real_part], axis=2)
    return jnp.stack([upper_part, lower_part], axis=2)


def weighted_rows(weights, selected):
    mode_count = weights.shape[1]
    total = None
    for mode_index in range(mode_count):
        for part_index in range(2):
            for direction in range(3):
                factor = jnp.transpose(
                    weights[:, mode_index, :, part_index, direction, :, :], (0, 2, 1, 3)
                )
                slab = selected[direction, :, mode_index, part_index].astype(jnp.float32)
                term = factor[:, None, :, :, :, None] * slab[None, :, None, None, :, :]
                total = term if total is None else total + term
    return total.astype(jnp.bfloat16)


def point_terms(source, chosen, derivative, offsets, targets, levels, flipped):
    blocks = jnp.einsum(
        "iab,scbd->iscad", derivative, source, preferred_element_type=jnp.float32
    ).astype(jnp.bfloat16)
    mode_count = chosen.shape[1]
    selected = jnp.stack(
        [
            lax.dynamic_slice_in_dim(blocks, levels - offsets[mode_index], targets, 1)
            for mode_index in range(mode_count)
        ],
        axis=2,
    )
    weights = mode_weights(chosen)
    combined = weighted_rows(weights, selected)
    sigma_part = jnp.einsum(
        "ktjxab,jbd->ktxad", combined, derivative, preferred_element_type=jnp.float32
    )
    polar_part = jnp.einsum(
        "itmcab,kticab->kmia", selected, flipped, preferred_element_type=jnp.float32
    )
    return (sigma_part, polar_part)


def per_device(green_blocks, derivative, bare_phonon, prior_polar, offsets, momenta):
    points = green_blocks.shape[0]
    levels = green_blocks.shape[1]
    block_order = green_blocks.shape[-1]
    all_points = points * lax.axis_size("mom")
    all_levels = levels * lax.axis_size("sec") * lax.axis_size("en")
    phonon = dyson_update(bare_phonon, prior_polar)
    local_modes = phonon.shape[0]
    stacked = phonon.reshape((local_modes * points,) + phonon.shape[2:])
    gathered = lax.all_gather(stacked, ("sec", "mom"), axis=0, tiled=True)
    mode_count = gathered.shape[0] // all_points
    phonon_table = jnp.transpose(
        gathered.reshape((mode_count, all_points) + phonon.shape[2:]), (1, 0, 2, 3, 4, 5)
    )
    own_rows = lax.dynamic_slice_in_dim(momenta, lax.axis_index("mom") * points, points, 0)
    momentum_ids = lax.broadcasted_iota(jnp.int32, (points, all_points), 1)
    lower_rim = passed_along(green_blocks, ("sec", "en"), 1)
    travelling = jnp.concatenate([lower_rim, green_blocks], axis=1)
    targets = green_blocks.shape[1]
    flipped = flipped_products(green_blocks, derivative)
    initial = (
        jnp.zeros((points, targets, 2, block_order, block_order), jnp.float32),
        jnp.zeros((all_points, mode_count, 3, block_order), jnp.float32),
    )
    pieces = lax.all_gather(travelling, "mom", axis=0, tiled=True)

    def one_point(position, running):
        sigma_sum, polar_sum = running
        source = lax.dynamic_index_in_dim(pieces, position, 0, keepdims=False)
        column = lax.dynamic_index_in_dim(own_rows, position, 1, keepdims=False)
        onehot = (column[:, None] == momentum_ids).astype(jnp.float32)
        chosen = jnp.einsum(
            "kq,qmxija->kmxija", onehot, phonon_table, precision=lax.Precision.HIGHEST
        )
        sigma_part, polar_part = point_terms(
            source, chosen, derivative, offsets, targets, levels, flipped
        )
        polar_sum = polar_sum + jnp.einsum(
            "kq,kmia->qmia", onehot, polar_part, precision=lax.Precision.HIGHEST
        )
        return (sigma_sum + sigma_part, polar_sum)

    sigma_sum, polar_sum = lax.fori_loop(0, pieces.shape[0], one_point, initial)
    sigma_scale = 1.0 / math.sqrt(9.0 * mode_count * all_points)
    polar_scale = 1.0 / math.sqrt(float(all_points * all_levels * block_order))
    ordered = jnp.transpose(polar_sum, (1, 0, 2, 3))
    summed = lax.psum(ordered, ("sec", "mom", "en"))
    own_share = lax.dynamic_slice(
        summed,
        (lax.axis_index("sec") * local_modes, lax.axis_index("mom") * points, 0, 0),
        (local_modes, points, 3, block_order),
    )
    return (sigma_sum * sigma_scale, own_share * polar_scale)


def solution(mesh):
    return jax.shard_map(
        per_device,
        mesh=mesh,
        in_specs=(
            P("mom", ("sec", "en"), None, None, None),
            P(),
            P("sec", "mom", None, None, None, None),
            P("sec", "mom", None, None, None, None),
            P(),
            P(),
        ),
        out_specs=(P("mom", ("sec", "en"), None, None, None), P("sec", "mom", None, None)),
        check_vma=False,
    )
```

profile of v0, /device:TPU:1, one launch (start us, length us, event | category | flops | bytes accessed | tf_op | source)
XLA Modules:
  0.0 422.1 jit_solution(5566107944990981499)
XLA Ops:
  7.3 4.5 %collective-permute-start = (bf16[1,2,2,128,128]{4,3,2,1,0:T(8,128)(2,1)}, bf16[1,2,2,128,128]{4,3,2,1,0:T(8,128)(2,1)S(1)}, u32[]{:S(2)}, u32[]{:S(2)}) collective-permute-start(bf16[1,2,2,128,128]{4,3,2,1,0:T(8,128)(2,1)} %param.9), channel_id=1, source_target_pairs={{0,1},{1,2},{2,3},{3,4},{4,5},{5,6},{6,7},{7,64},{64,65},{65,66},{... | collective-permute-start | bytes 393224 | tf_op jit(solution)/shard_map/ppermute | solution.py:11
  11.8 7.9 %collective-permute-done = bf16[1,2,2,128,128]{4,3,2,1,0:T(8,128)(2,1)S(1)} collective-permute-done((bf16[1,2,2,128,128]{4,3,2,1,0:T(8,128)(2,1)}, bf16[1,2,2,128,128]{4,3,2,1,0:T(8,128)(2,1)S(1)}, u32[]{:S(2)}, u32[]{:S(2)}) %collective-permute-start) | collective-permute-done | bytes 131104 | tf_op jit(solution)/shard_map/ppermute | solution.py:11
  19.7 1.6 pad_maximum_fusion.1
  21.3 1.5 fusion.141
  27.9 0.8 fusion.139
  28.7 0.8 fusion.140
  30.5 69.0 %all-gather = f32[32,1,2,3,3,128]{5,2,4,3,1,0:T(2,128)S(1)} all-gather(f32[1,1,2,3,3,128]{5,2,4,3,1,0:T(2,128)S(1)} %copy.131), channel_id=2, replica_groups=mesh['sec'=4,'mom'=8,'en'=8] {'sec','mom'}, dimensions={0}, use_global_device_ids=true | all-gather | bytes 304128 | tf_op jit(solution)/shard_map/all_gather | solution.py:95
  100.7 235.9 %while.19 = (s32[]{:T(128)}, f32[1,2,2,128,128]{4,3,2,1,0:T(8,128)}, f32[8,4,3,128]{3,2,1,0:T(4,128)}, s32[1,8]{1,0:T(1,128)}, f32[8,4,2,3,3,128]{5,4,3,2,1,0:T(...) while((s32[]{:T(128)}, ...), condition=%wide.region_9.10_spmd.clone, body=%wide.region_8.9_spmd.clone.sunk | while | flops 167619600 | bytes 31974176 | solution.py:128
  100.7 1.3 constant_dynamic-slice_fusion.3
  102.0 1.3 bitcast_convert_fusion.5
  103.3 1.1 fusion.161
  105.8 1.4 convolution_convert_fusion.2
  110.9 0.8 copy.223
  114.0 0.8 copy.227
  123.1 6.8 %fusion.167 = f32[1,2,2,128,128]{4,3,2,1,0:T(8,128)} fusion(f32[2,128,128]{2,1,0:T(8,128)S(1)} %copy-done.12, f32[3,2,128]{2,0,1:T(4,128)S(1)} %get-tuple-element.669, f32[2,128,128]{2,1,0:T(8,128)S(1)} %copy-done.13, f32[3,2,128]{2,0,1:T(4,128)S(1)} %get-tuple-element.671, f32[2,128,128]{2,1,0:T(8,128)} %copy.209, ...), kind=kOutput, calls=%fused_computation.5.clone.1 | convolution fusion | flops 59899904 | bytes 3842049 | tf_op jit(solution)/shard_map/while/body/eval_jaxpr/ktjxab,jbd->ktxad/dot_general | solution.py:77
  129.9 1.3 constant_dynamic-slice_fusion.3
  131.3 1.3 bitcast_convert_fusion.5
  132.5 1.1 fusion.161
  135.0 1.4 convolution_convert_fusion.2
  140.2 0.8 copy.223
  143.2 0.8 copy.227
  152.4 7.1 %fusion.167 = f32[1,2,2,128,128]{4,3,2,1,0:T(8,128)} fusion(f32[2,128,128]{2,1,0:T(8,128)S(1)} %copy-done.12, f32[3,2,128]{2,0,1:T(4,128)S(1)} %get-tuple-element.669, f32[2,128,128]{2,1,0:T(8,128)S(1)} %copy-done.13, f32[3,2,128]{2,0,1:T(4,128)S(1)} %get-tuple-element.671, f32[2,128,128]{2,1,0:T(8,128)} %copy.209, ...), kind=kOutput, calls=%fused_computation.5.clone.1 | convolution fusion | flops 59899904 | bytes 3842049 | tf_op jit(solution)/shard_map/while/body/eval_jaxpr/ktjxab,jbd->ktxad/dot_general | solution.py:77
  159.4 1.3 constant_dynamic-slice_fusion.3
  160.8 1.3 bitcast_convert_fusion.5
  162.1 1.1 fusion.161
  164.5 1.4 convolution_convert_fusion.2
  169.7 0.8 copy.223
  172.7 0.8 copy.227
  181.9 7.1 %fusion.167 = f32[1,2,2,128,128]{4,3,2,1,0:T(8,128)} fusion(f32[2,128,128]{2,1,0:T(8,128)S(1)} %copy-done.12, f32[3,2,128]{2,0,1:T(4,128)S(1)} %get-tuple-element.669, f32[2,128,128]{2,1,0:T(8,128)S(1)} %copy-done.13, f32[3,2,128]{2,0,1:T(4,128)S(1)} %get-tuple-element.671, f32[2,128,128]{2,1,0:T(8,128)} %copy.209, ...), kind=kOutput, calls=%fused_computation.5.clone.1 | convolution fusion | flops 59899904 | bytes 3842049 | tf_op jit(solution)/shard_map/while/body/eval_jaxpr/ktjxab,jbd->ktxad/dot_general | solution.py:77
  189.0 1.3 constant_dynamic-slice_fusion.3
  190.3 1.3 bitcast_convert_fusion.5
  191.6 1.1 fusion.161
  194.1 1.3 convolution_convert_fusion.2
  199.2 0.8 copy.223
  202.2 0.8 copy.227
  211.4 7.1 %fusion.167 = f32[1,2,2,128,128]{4,3,2,1,0:T(8,128)} fusion(f32[2,128,128]{2,1,0:T(8,128)S(1)} %copy-done.12, f32[3,2,128]{2,0,1:T(4,128)S(1)} %get-tuple-element.669, f32[2,128,128]{2,1,0:T(8,128)S(1)} %copy-done.13, f32[3,2,128]{2,0,1:T(4,128)S(1)} %get-tuple-element.671, f32[2,128,128]{2,1,0:T(8,128)} %copy.209, ...), kind=kOutput, calls=%fused_computation.5.clone.1 | convolution fusion | flops 59899904 | bytes 3842049 | tf_op jit(solution)/shard_map/while/body/eval_jaxpr/ktjxab,jbd->ktxad/dot_general | solution.py:77
  218.5 1.3 constant_dynamic-slice_fusion.3
  219.8 1.3 bitcast_convert_fusion.5
  221.1 1.1 fusion.161
  223.6 1.4 convolution_convert_fusion.2
  231.8 0.8 copy.227
  240.9 7.1 %fusion.167 = f32[1,2,2,128,128]{4,3,2,1,0:T(8,128)} fusion(f32[2,128,128]{2,1,0:T(8,128)S(1)} %copy-done.12, f32[3,2,128]{2,0,1:T(4,128)S(1)} %get-tuple-element.669, f32[2,128,128]{2,1,0:T(8,128)S(1)} %copy-done.13, f32[3,2,128]{2,0,1:T(4,128)S(1)} %get-tuple-element.671, f32[2,128,128]{2,1,0:T(8,128)} %copy.209, ...), kind=kOutput, calls=%fused_computation.5.clone.1 | convolution fusion | flops 59899904 | bytes 3842049 | tf_op jit(solution)/shard_map/while/body/eval_jaxpr/ktjxab,jbd->ktxad/dot_general | solution.py:77
  248.0 1.3 constant_dynamic-slice_fusion.3
  249.3 1.3 bitcast_convert_fusion.5
  250.6 1.1 fusion.161
  253.1 1.4 convolution_convert_fusion.2
  261.3 0.8 copy.227
  270.5 7.1 %fusion.167 = f32[1,2,2,128,128]{4,3,2,1,0:T(8,128)} fusion(f32[2,128,128]{2,1,0:T(8,128)S(1)} %copy-done.12, f32[3,2,128]{2,0,1:T(4,128)S(1)} %get-tuple-element.669, f32[2,128,128]{2,1,0:T(8,128)S(1)} %copy-done.13, f32[3,2,128]{2,0,1:T(4,128)S(1)} %get-tuple-element.671, f32[2,128,128]{2,1,0:T(8,128)} %copy.209, ...), kind=kOutput, calls=%fused_computation.5.clone.1 | convolution fusion | flops 59899904 | bytes 3842049 | tf_op jit(solution)/shard_map/while/body/eval_jaxpr/ktjxab,jbd->ktxad/dot_general | solution.py:77
  277.5 1.3 constant_dynamic-slice_fusion.3
  278.9 1.3 bitcast_convert_fusion.5
  280.1 1.1 fusion.161
  282.6 1.4 convolution_convert_fusion.2
  287.8 0.8 copy.223
  290.8 0.8 copy.227
  300.0 7.1 %fusion.167 = f32[1,2,2,128,128]{4,3,2,1,0:T(8,128)} fusion(f32[2,128,128]{2,1,0:T(8,128)S(1)} %copy-done.12, f32[3,2,128]{2,0,1:T(4,128)S(1)} %get-tuple-element.669, f32[2,128,128]{2,1,0:T(8,128)S(1)} %copy-done.13, f32[3,2,128]{2,0,1:T(4,128)S(1)} %get-tuple-element.671, f32[2,128,128]{2,1,0:T(8,128)} %copy.209, ...), kind=kOutput, calls=%fused_computation.5.clone.1 | convolution fusion | flops 59899904 | bytes 3842049 | tf_op jit(solution)/shard_map/while/body/eval_jaxpr/ktjxab,jbd->ktxad/dot_general | solution.py:77
  307.1 1.3 constant_dynamic-slice_fusion.3
  308.4 1.3 bitcast_convert_fusion.5
  309.7 1.1 fusion.161
  312.1 1.4 convolution_convert_fusion.2
  320.3 0.8 copy.227
  329.5 7.1 %fusion.167 = f32[1,2,2,128,128]{4,3,2,1,0:T(8,128)} fusion(f32[2,128,128]{2,1,0:T(8,128)S(1)} %copy-done.12, f32[3,2,128]{2,0,1:T(4,128)S(1)} %get-tuple-element.669, f32[2,128,128]{2,1,0:T(8,128)S(1)} %copy-done.13, f32[3,2,128]{2,0,1:T(4,128)S(1)} %get-tuple-element.671, f32[2,128,128]{2,1,0:T(8,128)} %copy.209, ...), kind=kOutput, calls=%fused_computation.5.clone.1 | convolution fusion | flops 59899904 | bytes 3842049 | tf_op jit(solution)/shard_map/while/body/eval_jaxpr/ktjxab,jbd->ktxad/dot_general | solution.py:77
  336.6 0.9 copy.175
  337.4 75.5 %psum.7 = f32[4,8,3,128]{3,1,2,0:T(8,128)S(1)} all-reduce(f32[4,8,3,128]{3,1,2,0:T(8,128)S(1)} %bitcast.412), channel_id=1, replica_groups=mesh['sec'=4,'mom'=8,'en'=8] {'sec','mom','en'}, use_global_device_ids=true, to_apply=%region_10.11 | all-reduce | flops 12288 | bytes 98304 | tf_op jit(solution)/shard_map/psum | solution.py:132
  413.0 1.7 broadcast_multiply_fusion
  (560 shorter events, 129.1 us)
Async XLA Ops:
  7.2 92.9 %copy-start = (s32[8,8]{1,0:T(8,128)S(1)}, s32[8,8]{1,0:T(8,128)}, u32[]{:S(2)}) copy-start(s32[8,8]{1,0:T(8,128)} %param.14) | copy-start | bytes 772
  7.2 92.5 %copy-start.18 = (f32[2]{0:T(128)S(1)}, f32[2]{0:T(128)}, u32[]{:S(2)}) copy-start(f32[2]{0:T(128)} %constant.97.clone) | copy-start | bytes 28
  7.2 92.5 %copy-start.16 = (bf16[1,2,2,128,128]{4,3,2,1,0:T(8,128)(2,1)S(1)}, bf16[1,2,2,128,128]{4,3,2,1,0:T(8,128)(2,1)}, u32[]{:S(2)}) copy-start(bf16[1,2,2,128,128]{4,3,2,1,0:T(8,128)(2,1)} %param.9) | copy-start | bytes 393220
  7.2 92.5 %copy-start.1 = (bf16[3,128,128]{2,1,0:T(8,128)(2,1)S(1)}, bf16[3,128,128]{2,1,0:T(8,128)(2,1)}, u32[]{:S(2)}) copy-start(bf16[3,128,128]{2,1,0:T(8,128)(2,1)} %param.10) | copy-start | bytes 294916
  7.2 93.5 %all-gather.3.cloned.1.call-start = ((), (), s32[]{:S(2)}) async-start(), calls=%async_computation | async-start | bytes 2359296 | tf_op jit(solution)/shard_map/all_gather | solution.py:110
  7.3 12.4 %collective-permute-start = (bf16[1,2,2,128,128]{4,3,2,1,0:T(8,128)(2,1)}, bf16[1,2,2,128,128]{4,3,2,1,0:T(8,128)(2,1)S(1)}, u32[]{:S(2)}, u32[]{:S(2)}) collective-permute-start(bf16[1,2,2,128,128]{4,3,2,1,0:T(8,128)(2,1)} %param.9), channel_id=1, source_target_pairs={{0,1},{1,2},{2,3},{3,4},{4,5},{5,6},{6,7},{7,64},{64,65},{65,66},{... | collective-permute-start | bytes 393224 | tf_op jit(solution)/shard_map/ppermute | solution.py:11
  117.1 5.9 %copy-start.2 = (f32[2,128,128]{2,1,0:T(8,128)S(1)}, f32[2,128,128]{2,1,0:T(8,128)}, u32[]{:S(2)}) copy-start(f32[2,128,128]{2,1,0:T(8,128)} %copy.221) | copy-start | bytes 393220 | tf_op jit(solution)/shard_map/while
  117.2 5.9 %copy-start.3 = (f32[2,128,128]{2,1,0:T(8,128)S(1)}, f32[2,128,128]{2,1,0:T(8,128)}, u32[]{:S(2)}) copy-start(f32[2,128,128]{2,1,0:T(8,128)} %copy.222) | copy-start | bytes 393220 | tf_op jit(solution)/shard_map/while
  117.2 5.9 %copy-start.4 = (f32[2,128,128]{2,1,0:T(8,128)S(1)}, f32[2,128,128]{2,1,0:T(8,128)}, u32[]{:S(2)}) copy-start(f32[2,128,128]{2,1,0:T(8,128)} %copy.223) | copy-start | bytes 393220 | tf_op jit(solution)/shard_map/while
  117.2 5.9 %copy-start.5 = (f32[2,128,128]{2,1,0:T(8,128)S(1)}, f32[2,128,128]{2,1,0:T(8,128)}, u32[]{:S(2)}) copy-start(f32[2,128,128]{2,1,0:T(8,128)} %copy.224) | copy-start | bytes 393220 | tf_op jit(solution)/shard_map/while
  117.2 5.9 %copy-start.6 = (f32[2,128,128]{2,1,0:T(8,128)S(1)}, f32[2,128,128]{2,1,0:T(8,128)}, u32[]{:S(2)}) copy-start(f32[2,128,128]{2,1,0:T(8,128)} %copy.225) | copy-start | bytes 393220 | tf_op jit(solution)/shard_map/while
  117.2 5.9 %copy-start.7 = (f32[2,128,128]{2,1,0:T(8,128)S(1)}, f32[2,128,128]{2,1,0:T(8,128)}, u32[]{:S(2)}) copy-start(f32[2,128,128]{2,1,0:T(8,128)} %copy.226) | copy-start | bytes 393220 | tf_op jit(solution)/shard_map/while
  118.0 5.1 %copy-start.8 = (f32[2,128,128]{2,1,0:T(8,128)S(1)}, f32[2,128,128]{2,1,0:T(8,128)}, u32[]{:S(2)}) copy-start(f32[2,128,128]{2,1,0:T(8,128)} %copy.227) | copy-start | bytes 393220 | tf_op jit(solution)/shard_map/while
  146.4 5.9 %copy-start.2 = (f32[2,128,128]{2,1,0:T(8,128)S(1)}, f32[2,128,128]{2,1,0:T(8,128)}, u32[]{:S(2)}) copy-start(f32[2,128,128]{2,1,0:T(8,128)} %copy.221) | copy-start | bytes 393220 | tf_op jit(solution)/shard_map/while
  146.4 5.9 %copy-start.3 = (f32[2,128,128]{2,1,0:T(8,128)S(1)}, f32[2,128,128]{2,1,0:T(8,128)}, u32[]{:S(2)}) copy-start(f32[2,128,128]{2,1,0:T(8,128)} %copy.222) | copy-start | bytes 393220 | tf_op jit(solution)/shard_map/while
  146.4 5.9 %copy-start.4 = (f32[2,128,128]{2,1,0:T(8,128)S(1)}, f32[2,128,128]{2,1,0:T(8,128)}, u32[]{:S(2)}) copy-start(f32[2,128,128]{2,1,0:T(8,128)} %copy.223) | copy-start | bytes 393220 | tf_op jit(solution)/shard_map/while
  146.4 5.9 %copy-start.5 = (f32[2,128,128]{2,1,0:T(8,128)S(1)}, f32[2,128,128]{2,1,0:T(8,128)}, u32[]{:S(2)}) copy-start(f32[2,128,128]{2,1,0:T(8,128)} %copy.224) | copy-start | bytes 393220 | tf_op jit(solution)/shard_map/while
  146.4 5.9 %copy-start.6 = (f32[2,128,128]{2,1,0:T(8,128)S(1)}, f32[2,128,128]{2,1,0:T(8,128)}, u32[]{:S(2)}) copy-start(f32[2,128,128]{2,1,0:T(8,128)} %copy.225) | copy-start | bytes 393220 | tf_op jit(solution)/shard_map/while
  146.4 5.9 %copy-start.7 = (f32[2,128,128]{2,1,0:T(8,128)S(1)}, f32[2,128,128]{2,1,0:T(8,128)}, u32[]{:S(2)}) copy-start(f32[2,128,128]{2,1,0:T(8,128)} %copy.226) | copy-start | bytes 393220 | tf_op jit(solution)/shard_map/while
  147.2 5.1 %copy-start.8 = (f32[2,128,128]{2,1,0:T(8,128)S(1)}, f32[2,128,128]{2,1,0:T(8,128)}, u32[]{:S(2)}) copy-start(f32[2,128,128]{2,1,0:T(8,128)} %copy.227) | copy-start | bytes 393220 | tf_op jit(solution)/shard_map/while
  148.0 4.4 %copy-start.9 = (f32[2,128,128]{2,1,0:T(8,128)S(1)}, f32[2,128,128]{2,1,0:T(8,128)}, u32[]{:S(2)}) copy-start(f32[2,128,128]{2,1,0:T(8,128)} %copy.228) | copy-start | bytes 393220 | tf_op jit(solution)/shard_map/while
  175.9 5.9 %copy-start.2 = (f32[2,128,128]{2,1,0:T(8,128)S(1)}, f32[2,128,128]{2,1,0:T(8,128)}, u32[]{:S(2)}) copy-start(f32[2,128,128]{2,1,0:T(8,128)} %copy.221) | copy-start | bytes 393220 | tf_op jit(solution)/shard_map/while
  175.9 5.9 %copy-start.3 = (f32[2,128,128]{2,1,0:T(8,128)S(1)}, f32[2,128,128]{2,1,0:T(8,128)}, u32[]{:S(2)}) copy-start(f32[2,128,128]{2,1,0:T(8,128)} %copy.222) | copy-start | bytes 393220 | tf_op jit(solution)/shard_map/while
  175.9 5.9 %copy-start.4 = (f32[2,128,128]{2,1,0:T(8,128)S(1)}, f32[2,128,128]{2,1,0:T(8,128)}, u32[]{:S(2)}) copy-start(f32[2,128,128]{2,1,0:T(8,128)} %copy.223) | copy-start | bytes 393220 | tf_op jit(solution)/shard_map/while
  175.9 5.9 %copy-start.5 = (f32[2,128,128]{2,1,0:T(8,128)S(1)}, f32[2,128,128]{2,1,0:T(8,128)}, u32[]{:S(2)}) copy-start(f32[2,128,128]{2,1,0:T(8,128)} %copy.224) | copy-start | bytes 393220 | tf_op jit(solution)/shard_map/while
  175.9 5.9 %copy-start.6 = (f32[2,128,128]{2,1,0:T(8,128)S(1)}, f32[2,128,128]{2,1,0:T(8,128)}, u32[]{:S(2)}) copy-start(f32[2,128,128]{2,1,0:T(8,128)} %copy.225) | copy-start | bytes 393220 | tf_op jit(solution)/shard_map/while
  176.0 5.9 %copy-start.7 = (f32[2,128,128]{2,1,0:T(8,128)S(1)}, f32[2,128,128]{2,1,0:T(8,128)}, u32[]{:S(2)}) copy-start(f32[2,128,128]{2,1,0:T(8,128)} %copy.226) | copy-start | bytes 393220 | tf_op jit(solution)/shard_map/while
  176.7 5.1 %copy-start.8 = (f32[2,128,128]{2,1,0:T(8,128)S(1)}, f32[2,128,128]{2,1,0:T(8,128)}, u32[]{:S(2)}) copy-start(f32[2,128,128]{2,1,0:T(8,128)} %copy.227) | copy-start | bytes 393220 | tf_op jit(solution)/shard_map/while
  205.4 5.9 %copy-start.2 = (f32[2,128,128]{2,1,0:T(8,128)S(1)}, f32[2,128,128]{2,1,0:T(8,128)}, u32[]{:S(2)}) copy-start(f32[2,128,128]{2,1,0:T(8,128)} %copy.221) | copy-start | bytes 393220 | tf_op jit(solution)/shard_map/while
  205.4 5.9 %copy-start.3 = (f32[2,128,128]{2,1,0:T(8,128)S(1)}, f32[2,128,128]{2,1,0:T(8,128)}, u32[]{:S(2)}) copy-start(f32[2,128,128]{2,1,0:T(8,128)} %copy.222) | copy-start | bytes 393220 | tf_op jit(solution)/shard_map/while
  205.4 5.9 %copy-start.4 = (f32[2,128,128]{2,1,0:T(8,128)S(1)}, f32[2,128,128]{2,1,0:T(8,128)}, u32[]{:S(2)}) copy-start(f32[2,128,128]{2,1,0:T(8,128)} %copy.223) | copy-start | bytes 393220 | tf_op jit(solution)/shard_map/while
  205.5 5.9 %copy-start.5 = (f32[2,128,128]{2,1,0:T(8,128)S(1)}, f32[2,128,128]{2,1,0:T(8,128)}, u32[]{:S(2)}) copy-start(f32[2,128,128]{2,1,0:T(8,128)} %copy.224) | copy-start | bytes 393220 | tf_op jit(solution)/shard_map/while
  205.5 5.9 %copy-start.6 = (f32[2,128,128]{2,1,0:T(8,128)S(1)}, f32[2,128,128]{2,1,0:T(8,128)}, u32[]{:S(2)}) copy-start(f32[2,128,128]{2,1,0:T(8,128)} %copy.225) | copy-start | bytes 393220 | tf_op jit(solution)/shard_map/while
  205.5 5.9 %copy-start.7 = (f32[2,128,128]{2,1,0:T(8,128)S(1)}, f32[2,128,128]{2,1,0:T(8,128)}, u32[]{:S(2)}) copy-start(f32[2,128,128]{2,1,0:T(8,128)} %copy.226) | copy-start | bytes 393220 | tf_op jit(solution)/shard_map/while
  206.2 5.1 %copy-start.8 = (f32[2,128,128]{2,1,0:T(8,128)S(1)}, f32[2,128,128]{2,1,0:T(8,128)}, u32[]{:S(2)}) copy-start(f32[2,128,128]{2,1,0:T(8,128)} %copy.227) | copy-start | bytes 393220 | tf_op jit(solution)/shard_map/while
  207.0 4.4 %copy-start.9 = (f32[2,128,128]{2,1,0:T(8,128)S(1)}, f32[2,128,128]{2,1,0:T(8,128)}, u32[]{:S(2)}) copy-start(f32[2,128,128]{2,1,0:T(8,128)} %copy.228) | copy-start | bytes 393220 | tf_op jit(solution)/shard_map/while
  234.9 5.9 %copy-start.2 = (f32[2,128,128]{2,1,0:T(8,128)S(1)}, f32[2,128,128]{2,1,0:T(8,128)}, u32[]{:S(2)}) copy-start(f32[2,128,128]{2,1,0:T(8,128)} %copy.221) | copy-start | bytes 393220 | tf_op jit(solution)/shard_map/while
  235.0 5.9 %copy-start.3 = (f32[2,128,128]{2,1,0:T(8,128)S(1)}, f32[2,128,128]{2,1,0:T(8,128)}, u32[]{:S(2)}) copy-start(f32[2,128,128]{2,1,0:T(8,128)} %copy.222) | copy-start | bytes 393220 | tf_op jit(solution)/shard_map/while
  235.0 5.9 %copy-start.4 = (f32[2,128,128]{2,1,0:T(8,128)S(1)}, f32[2,128,128]{2,1,0:T(8,128)}, u32[]{:S(2)}) copy-start(f32[2,128,128]{2,1,0:T(8,128)} %copy.223) | copy-start | bytes 393220 | tf_op jit(solution)/shard_map/while
  235.0 5.9 %copy-start.5 = (f32[2,128,128]{2,1,0:T(8,128)S(1)}, f32[2,128,128]{2,1,0:T(8,128)}, u32[]{:S(2)}) copy-start(f32[2,128,128]{2,1,0:T(8,128)} %copy.224) | copy-start | bytes 393220 | tf_op jit(solution)/shard_map/while
  235.0 5.9 %copy-start.6 = (f32[2,128,128]{2,1,0:T(8,128)S(1)}, f32[2,128,128]{2,1,0:T(8,128)}, u32[]{:S(2)}) copy-start(f32[2,128,128]{2,1,0:T(8,128)} %copy.225) | copy-start | bytes 393220 | tf_op jit(solution)/shard_map/while
  235.0 5.9 %copy-start.7 = (f32[2,128,128]{2,1,0:T(8,128)S(1)}, f32[2,128,128]{2,1,0:T(8,128)}, u32[]{:S(2)}) copy-start(f32[2,128,128]{2,1,0:T(8,128)} %copy.226) | copy-start | bytes 393220 | tf_op jit(solution)/shard_map/while
  235.8 5.1 %copy-start.8 = (f32[2,128,128]{2,1,0:T(8,128)S(1)}, f32[2,128,128]{2,1,0:T(8,128)}, u32[]{:S(2)}) copy-start(f32[2,128,128]{2,1,0:T(8,128)} %copy.227) | copy-start | bytes 393220 | tf_op jit(solution)/shard_map/while
  264.5 5.9 %copy-start.2 = (f32[2,128,128]{2,1,0:T(8,128)S(1)}, f32[2,128,128]{2,1,0:T(8,128)}, u32[]{:S(2)}) copy-start(f32[2,128,128]{2,1,0:T(8,128)} %copy.221) | copy-start | bytes 393220 | tf_op jit(solution)/shard_map/while
  264.5 5.9 %copy-start.3 = (f32[2,128,128]{2,1,0:T(8,128)S(1)}, f32[2,128,128]{2,1,0:T(8,128)}, u32[]{:S(2)}) copy-start(f32[2,128,128]{2,1,0:T(8,128)} %copy.222) | copy-start | bytes 393220 | tf_op jit(solution)/shard_map/while
  264.5 5.9 %copy-start.4 = (f32[2,128,128]{2,1,0:T(8,128)S(1)}, f32[2,128,128]{2,1,0:T(8,128)}, u32[]{:S(2)}) copy-start(f32[2,128,128]{2,1,0:T(8,128)} %copy.223) | copy-start | bytes 393220 | tf_op jit(solution)/shard_map/while
  264.5 5.9 %copy-start.5 = (f32[2,128,128]{2,1,0:T(8,128)S(1)}, f32[2,128,128]{2,1,0:T(8,128)}, u32[]{:S(2)}) copy-start(f32[2,128,128]{2,1,0:T(8,128)} %copy.224) | copy-start | bytes 393220 | tf_op jit(solution)/shard_map/while
  264.5 5.9 %copy-start.6 = (f32[2,128,128]{2,1,0:T(8,128)S(1)}, f32[2,128,128]{2,1,0:T(8,128)}, u32[]{:S(2)}) copy-start(f32[2,128,128]{2,1,0:T(8,128)} %copy.225) | copy-start | bytes 393220 | tf_op jit(solution)/shard_map/while
  264.5 5.9 %copy-start.7 = (f32[2,128,128]{2,1,0:T(8,128)S(1)}, f32[2,128,128]{2,1,0:T(8,128)}, u32[]{:S(2)}) copy-start(f32[2,128,128]{2,1,0:T(8,128)} %copy.226) | copy-start | bytes 393220 | tf_op jit(solution)/shard_map/while
  265.3 5.1 %copy-start.8 = (f32[2,128,128]{2,1,0:T(8,128)S(1)}, f32[2,128,128]{2,1,0:T(8,128)}, u32[]{:S(2)}) copy-start(f32[2,128,128]{2,1,0:T(8,128)} %copy.227) | copy-start | bytes 393220 | tf_op jit(solution)/shard_map/while
  294.0 5.9 %copy-start.2 = (f32[2,128,128]{2,1,0:T(8,128)S(1)}, f32[2,128,128]{2,1,0:T(8,128)}, u32[]{:S(2)}) copy-start(f32[2,128,128]{2,1,0:T(8,128)} %copy.221) | copy-start | bytes 393220 | tf_op jit(solution)/shard_map/while
  294.0 5.9 %copy-start.3 = (f32[2,128,128]{2,1,0:T(8,128)S(1)}, f32[2,128,128]{2,1,0:T(8,128)}, u32[]{:S(2)}) copy-start(f32[2,128,128]{2,1,0:T(8,128)} %copy.222) | copy-start | bytes 393220 | tf_op jit(solution)/shard_map/while
  294.0 5.9 %copy-start.4 = (f32[2,128,128]{2,1,0:T(8,128)S(1)}, f32[2,128,128]{2,1,0:T(8,128)}, u32[]{:S(2)}) copy-start(f32[2,128,128]{2,1,0:T(8,128)} %copy.223) | copy-start | bytes 393220 | tf_op jit(solution)/shard_map/while
  294.0 5.9 %copy-start.5 = (f32[2,128,128]{2,1,0:T(8,128)S(1)}, f32[2,128,128]{2,1,0:T(8,128)}, u32[]{:S(2)}) copy-start(f32[2,128,128]{2,1,0:T(8,128)} %copy.224) | copy-start | bytes 393220 | tf_op jit(solution)/shard_map/while
  294.0 5.9 %copy-start.6 = (f32[2,128,128]{2,1,0:T(8,128)S(1)}, f32[2,128,128]{2,1,0:T(8,128)}, u32[]{:S(2)}) copy-start(f32[2,128,128]{2,1,0:T(8,128)} %copy.225) | copy-start | bytes 393220 | tf_op jit(solution)/shard_map/while
  294.0 5.9 %copy-start.7 = (f32[2,128,128]{2,1,0:T(8,128)S(1)}, f32[2,128,128]{2,1,0:T(8,128)}, u32[]{:S(2)}) copy-start(f32[2,128,128]{2,1,0:T(8,128)} %copy.226) | copy-start | bytes 393220 | tf_op jit(solution)/shard_map/while
  294.8 5.1 %copy-start.8 = (f32[2,128,128]{2,1,0:T(8,128)S(1)}, f32[2,128,128]{2,1,0:T(8,128)}, u32[]{:S(2)}) copy-start(f32[2,128,128]{2,1,0:T(8,128)} %copy.227) | copy-start | bytes 393220 | tf_op jit(solution)/shard_map/while
  323.5 5.9 %copy-start.2 = (f32[2,128,128]{2,1,0:T(8,128)S(1)}, f32[2,128,128]{2,1,0:T(8,128)}, u32[]{:S(2)}) copy-start(f32[2,128,128]{2,1,0:T(8,128)} %copy.221) | copy-start | bytes 393220 | tf_op jit(solution)/shard_map/while
  323.5 5.9 %copy-start.3 = (f32[2,128,128]{2,1,0:T(8,128)S(1)}, f32[2,128,128]{2,1,0:T(8,128)}, u32[]{:S(2)}) copy-start(f32[2,128,128]{2,1,0:T(8,128)} %copy.222) | copy-start | bytes 393220 | tf_op jit(solution)/shard_map/while
  323.5 5.9 %copy-start.4 = (f32[2,128,128]{2,1,0:T(8,128)S(1)}, f32[2,128,128]{2,1,0:T(8,128)}, u32[]{:S(2)}) copy-start(f32[2,128,128]{2,1,0:T(8,128)} %copy.223) | copy-start | bytes 393220 | tf_op jit(solution)/shard_map/while
  323.5 5.9 %copy-start.5 = (f32[2,128,128]{2,1,0:T(8,128)S(1)}, f32[2,128,128]{2,1,0:T(8,128)}, u32[]{:S(2)}) copy-start(f32[2,128,128]{2,1,0:T(8,128)} %copy.224) | copy-start | bytes 393220 | tf_op jit(solution)/shard_map/while
  323.6 5.9 %copy-start.6 = (f32[2,128,128]{2,1,0:T(8,128)S(1)}, f32[2,128,128]{2,1,0:T(8,128)}, u32[]{:S(2)}) copy-start(f32[2,128,128]{2,1,0:T(8,128)} %copy.225) | copy-start | bytes 393220 | tf_op jit(solution)/shard_map/while
  323.6 5.9 %copy-start.7 = (f32[2,128,128]{2,1,0:T(8,128)S(1)}, f32[2,128,128]{2,1,0:T(8,128)}, u32[]{:S(2)}) copy-start(f32[2,128,128]{2,1,0:T(8,128)} %copy.226) | copy-start | bytes 393220 | tf_op jit(solution)/shard_map/while
  324.3 5.1 %copy-start.8 = (f32[2,128,128]{2,1,0:T(8,128)S(1)}, f32[2,128,128]{2,1,0:T(8,128)}, u32[]{:S(2)}) copy-start(f32[2,128,128]{2,1,0:T(8,128)} %copy.227) | copy-start | bytes 393220 | tf_op jit(solution)/shard_map/while
  (62 other events, 124.8 us)
Sparse Core Ops, SparseCore 0:
  21.4 60.3 all-gather.2
where the time goes:
time: 428 us; the launch traced here: 422 us
  blocking collectives  145 us (34%)
  local copies, waits for them, and re-layouts  135 us (32%)
  matrix products  76.3 us (18%)
  other arithmetic  31.9 us (7%)
  between operations  19.4 us (5%)
  waiting for transfers between devices  7.91 us (2%)
  starting transfers between devices  4.53 us (1%)
    mul x192, local copies, waits for them, and re-layouts, weighted_rows(): term = factor[:, None, :, :, :, None] * slab[None, :, None, None, :, :]  108 us
    psum x1, blocking collectives, per_device(): summed = lax.psum(ordered, ('sec', 'mom', 'en'))  75.5 us
    all_gather x1, blocking collectives, per_device(): gathered = lax.all_gather(stacked, ('sec', 'mom'), axis=0, tiled=True)  69 us
    dot_general x8, matrix products, point_terms(): jnp.einsum('ktjxab,jbd->ktxad', combined, derivative, preferred_element_t...  56.2 us
    mul x40, other arithmetic, weighted_rows(): term = factor[:, None, :, :, :, None] * slab[None, :, None, None, :, :]  12.7 us
    dot_general x8, matrix products, point_terms(): jnp.einsum('iab,scbd->iscad', derivative, source, preferred_element_type=...  10.8 us
    dynamic_slice x8, local copies, waits for them, and re-layouts, one_point(): column = lax.dynamic_index_in_dim(own_rows, position, 1, keepdims=False)  10.7 us
    another operation x8, other arithmetic  10.2 us
  transfers between devices with their start and end apart: 2, of which 1 were waited for; matrix products, arithmetic and copies ran while one was open for 1% of the time, Pallas kernels for 0%

commit v1 on v0

--- a/solution.py
+++ b/solution.py
@@ -1,8 +1,17 @@
+import functools
 import math
 import jax
 import jax.numpy as jnp
 from jax import lax
 from jax.sharding import PartitionSpec as P
+from jax.lax import all_gather
+
+
+def page_group(xs, axis_name):
+    return jnp.sum(all_gather(xs, axis_name=axis_name), axis=0)
+
+
+solve_strips_all = functools.partial(page_group, axis_name=("sec", "mom", "en"))
 
 
 def passed_along(x, axis, by):
@@ -129,7 +138,7 @@
     sigma_scale = 1.0 / math.sqrt(9.0 * mode_count * all_points)
     polar_scale = 1.0 / math.sqrt(float(all_points * all_levels * block_order))
     ordered = jnp.transpose(polar_sum, (1, 0, 2, 3))
-    summed = lax.psum(ordered, ("sec", "mom", "en"))
+    summed = solve_strips_all(ordered)
     own_share = lax.dynamic_slice(
         summed,
         (lax.axis_index("sec") * local_modes, lax.axis_index("mom") * points, 0, 0),

time: 428 us -> 1090 us (2.55)
  waiting for transfers between devices: 7.91 us -> 736 us
  blocking collectives: 145 us -> 68.7 us
    all_gather x0 -> x1, waiting for transfers between devices: none -> 728 us  [page_group(): return jnp.sum(all_gather(xs, axis_name=axis_name), axis=0)]
    psum x1 -> x0, blocking collectives: 75.5 us -> none  [per_device(): summed = lax.psum(ordered, ('sec', 'mom', 'en'))]
  transfers between devices with their start and end apart: 2 -> 3, of which waited for: 1 -> 2; matrix products, arithmetic and copies ran while one was open for 1% -> 1% of each run, Pallas kernels for 0% -> 0%
where the time goes in v1:
time: 1090 us; the launch traced here: 1080 us
  waiting for transfers between devices  736 us (68%)
  local copies, waits for them, and re-layouts  133 us (12%)
  matrix products  75.5 us (7%)
  blocking collectives  68.7 us (6%)
  other arithmetic  39.2 us (4%)
  between operations  19.4 us (2%)
    all_gather x1, waiting for transfers between devices, page_group(): return jnp.sum(all_gather(xs, axis_name=axis_name), axis=0)  728 us
    mul x192, local copies, waits for them, and re-layouts, weighted_rows(): term = factor[:, None, :, :, :, None] * slab[None, :, None, None, :, :]  107 us
    all_gather x1, blocking collectives, per_device(): gathered = lax.all_gather(stacked, ('sec', 'mom'), axis=0, tiled=True)  68.7 us
    dot_general x8, matrix products, point_terms(): jnp.einsum('ktjxab,jbd->ktxad', combined, derivative, preferred_element_t...  56.2 us
  transfers between devices with their start and end apart: 3, of which 2 were waited for; matrix products, arithmetic and copies ran while one was open for 1% of the time, Pallas kernels for 0%

profile of v1, /device:TPU:1, one launch (start us, length us, event | category | flops | bytes accessed | tf_op | source)
XLA Modules:
  0.0 1079.2 jit_solution(4417534991939315481)
XLA Ops:
  7.3 4.5 collective-permute-start
  11.8 7.9 collective-permute-done
  19.7 1.6 pad_maximum_fusion.1
  21.4 1.5 fusion.141
  28.0 0.8 fusion.139
  28.8 0.8 fusion.140
  30.5 68.7 %all-gather = f32[32,1,2,3,3,128]{5,2,4,3,1,0:T(2,128)S(1)} all-gather(f32[1,1,2,3,3,128]{5,2,4,3,1,0:T(2,128)S(1)} %copy.129), channel_id=2, replica_groups=mesh['sec'=4,'mom'=8,'en'=8] {'sec','mom'}, dimensions={0}, use_global_device_ids=true | all-gather | bytes 304128 | tf_op jit(solution)/shard_map/all_gather | solution.py:104
  100.4 232.6 %while.19 = (s32[]{:T(128)}, f32[1,2,2,128,128]{4,3,2,1,0:T(8,128)}, f32[8,4,3,128]{3,2,1,0:T(4,128)}, s32[1,8]{1,0:T(1,128)}, f32[8,4,2,3,3,128]{5,4,3,2,1,0:T(...) while((s32[]{:T(128)}, ...), condition=%wide.region_9.10_spmd.clone, body=%wide.region_8.9_spmd.clone.sunk | while | flops 167619600 | bytes 31974176 | solution.py:137
  100.4 1.3 constant_dynamic-slice_fusion.3
  101.7 1.1 bitcast_convert_fusion.5
  102.9 1.0 fusion.161
  105.3 1.3 convolution_convert_fusion.2
  113.4 0.8 copy.223
  116.6 0.8 copy.202
  122.5 6.8 fusion.167
  129.3 1.3 constant_dynamic-slice_fusion.3
  130.6 1.1 bitcast_convert_fusion.5
  131.7 1.0 fusion.161
  134.1 1.3 convolution_convert_fusion.2
  142.2 0.8 copy.223
  145.4 0.8 copy.202
  151.3 7.1 fusion.167
  158.4 1.3 constant_dynamic-slice_fusion.3
  159.7 1.1 bitcast_convert_fusion.5
  160.8 1.0 fusion.161
  163.2 1.3 convolution_convert_fusion.2
  171.3 0.8 copy.223
  174.6 0.8 copy.202
  180.4 7.1 fusion.167
  187.5 1.3 constant_dynamic-slice_fusion.3
  188.8 1.1 bitcast_convert_fusion.5
  189.9 1.0 fusion.161
  192.3 1.3 convolution_convert_fusion.2
  200.5 0.8 copy.223
  203.7 0.8 copy.202
  209.5 7.1 fusion.167
  216.6 1.3 constant_dynamic-slice_fusion.3
  217.9 1.1 bitcast_convert_fusion.5
  219.0 1.0 fusion.161
  221.4 1.3 convolution_convert_fusion.2
  229.6 0.8 copy.223
  232.8 0.8 copy.202
  238.7 7.1 fusion.167
  245.7 1.3 constant_dynamic-slice_fusion.3
  247.0 1.1 bitcast_convert_fusion.5
  248.2 1.0 fusion.161
  250.6 1.3 convolution_convert_fusion.2
  258.7 0.8 copy.223
  267.8 7.1 fusion.167
  274.9 1.3 constant_dynamic-slice_fusion.3
  276.1 1.1 bitcast_convert_fusion.5
  277.3 1.0 fusion.161
  279.7 1.3 convolution_convert_fusion.2
  287.8 0.8 copy.223
  296.9 7.1 fusion.167
  304.0 1.3 constant_dynamic-slice_fusion.3
  305.3 1.1 bitcast_convert_fusion.5
  306.4 1.0 fusion.161
  308.8 1.3 convolution_convert_fusion.2
  316.9 0.8 copy.223
  326.0 7.1 fusion.167
  333.1 1.7 broadcast_multiply_fusion
  334.8 728.2 %all-gather.7.cloned.1.call-done = f32[1024,8,3,128]{3,2,0,1:T(4,128)} async-done(((f32[4,8,3,128]{3,2,0,1:T(4,128)}), f32[1024,8,3,128]{3,2,0,1:T(4,128)}) %all-gather.7.cloned.1.call-update) | async-done | bytes 12582928 | tf_op jit(solution)/shard_map/all_gather | solution.py:11
  1062.9 8.8 reduce_sum.89
  (563 shorter events, 128.2 us)
Async XLA Ops:
  7.2 92.7 %copy-start = (s32[8,8]{1,0:T(8,128)S(1)}, s32[8,8]{1,0:T(8,128)}, u32[]{:S(2)}) copy-start(s32[8,8]{1,0:T(8,128)} %param.14) | copy-start | bytes 772
  7.2 92.3 %copy-start.18 = (f32[2]{0:T(128)S(1)}, f32[2]{0:T(128)}, u32[]{:S(2)}) copy-start(f32[2]{0:T(128)} %constant.97.clone) | copy-start | bytes 28
  7.2 92.3 %copy-start.16 = (bf16[1,2,2,128,128]{4,3,2,1,0:T(8,128)(2,1)S(1)}, bf16[1,2,2,128,128]{4,3,2,1,0:T(8,128)(2,1)}, u32[]{:S(2)}) copy-start(bf16[1,2,2,128,128]{4,3,2,1,0:T(8,128)(2,1)} %param.9) | copy-start | bytes 393220
  7.2 92.3 %copy-start.1 = (bf16[3,128,128]{2,1,0:T(8,128)(2,1)S(1)}, bf16[3,128,128]{2,1,0:T(8,128)(2,1)}, u32[]{:S(2)}) copy-start(bf16[3,128,128]{2,1,0:T(8,128)(2,1)} %param.10) | copy-start | bytes 294916
  7.2 93.2 %all-gather.5.cloned.1.call-start = ((), (), s32[]{:S(2)}) async-start(), calls=%async_computation | async-start | bytes 2359296 | tf_op jit(solution)/shard_map/all_gather | solution.py:119
  7.3 12.4 %collective-permute-start = (bf16[1,2,2,128,128]{4,3,2,1,0:T(8,128)(2,1)}, bf16[1,2,2,128,128]{4,3,2,1,0:T(8,128)(2,1)S(1)}, u32[]{:S(2)}, u32[]{:S(2)}) collective-permute-start(bf16[1,2,2,128,128]{4,3,2,1,0:T(8,128)(2,1)} %param.9), channel_id=1, source_target_pairs={{0,1},{1,2},{2,3},{3,4},{4,5},{5,6},{6,7},{7,64},{64,65},{65,66},{... | collective-permute-start | bytes 393224 | tf_op jit(solution)/shard_map/ppermute | solution.py:20
  21.3 1041.6 %all-gather.7.cloned.1.call-start = ((), (), s32[]{:S(2)}) async-start(), calls=%async_computation.1 | async-start | bytes 16842752 | tf_op jit(solution)/shard_map/all_gather | solution.py:11
  116.5 5.8 copy-start.2
  116.6 5.8 copy-start.3
  116.6 5.8 copy-start.4
  116.6 5.8 copy-start.5
  116.6 5.8 copy-start.6
  116.6 5.8 copy-start.7
  117.4 5.1 copy-start.8
  118.1 4.3 copy-start.9
  145.4 5.8 copy-start.2
  145.4 5.8 copy-start.3
  145.4 5.8 copy-start.4
  145.4 5.8 copy-start.5
  145.4 5.8 copy-start.6
  145.4 5.8 copy-start.7
  146.2 5.1 copy-start.8
  174.5 5.8 copy-start.2
  174.5 5.8 copy-start.3
  174.5 5.8 copy-start.4
  174.5 5.8 copy-start.5
  174.5 5.8 copy-start.6
  174.6 5.8 copy-start.7
  175.3 5.1 copy-start.8
  203.6 5.8 copy-start.2
  203.6 5.8 copy-start.3
  203.6 5.8 copy-start.4
  203.6 5.8 copy-start.5
  203.7 5.8 copy-start.6
  203.7 5.8 copy-start.7
  204.4 5.1 copy-start.8
  232.7 5.8 copy-start.2
  232.7 5.8 copy-start.3
  232.8 5.8 copy-start.4
  232.8 5.8 copy-start.5
  232.8 5.8 copy-start.6
  232.8 5.8 copy-start.7
  233.6 5.1 copy-start.8
  261.9 5.8 copy-start.2
  261.9 5.8 copy-start.3
  261.9 5.8 copy-start.4
  261.9 5.8 copy-start.5
  261.9 5.8 copy-start.6
  261.9 5.8 copy-start.7
  262.7 5.1 copy-start.8
  291.0 5.8 copy-start.2
  291.0 5.8 copy-start.3
  291.0 5.8 copy-start.4
  291.0 5.8 copy-start.5
  291.0 5.8 copy-start.6
  291.0 5.8 copy-start.7
  291.8 5.1 copy-start.8
  320.1 5.8 copy-start.2
  320.1 5.8 copy-start.3
  320.1 5.8 copy-start.4
  320.1 5.8 copy-start.5
  320.1 5.8 copy-start.6
  320.1 5.8 copy-start.7
  320.9 5.1 copy-start.8
  (63 other events, 127.7 us)
Sparse Core Ops, SparseCore 0:
  21.4 60.1 all-gather.4
  333.2 729.6 all-gather.6
